TPU v7x, 32 devices: a whole 2x2x4 slice. The times are simulated.
32 devices in a mesh: section: 4 (over x, core), ctx: 8 (over z, y).
Axes of the slice: x: 2, y: 2, z: 4, core: 2. Of those that a mesh axis runs over, the one named last changes fastest.
Arguments:
- tokens: bfloat16 [6144, 8192], P(('section', 'ctx')), may hold values from -60 to 60
- norm_gain: float32 [1, 2, 8192], replicated, may hold values from 0.1 to 1.9
- feat_taps: float32 [1, 2, 3, 3, 8192], replicated, may hold values from -3.5 to 3.5
- se_taps: float32 [1, 7, 8192], replicated, may hold values from -2 to 2
- mr_taps: bfloat16 [1, 128, 512], replicated, may hold values from -0.5 to 0.5
Outputs:
- final: bfloat16 [6144, 8192], P(('section', 'ctx'))
All inputs are finite; a program needn't handle non-finite values.
Results may differ from a plain program's by a relative error of at most 0.0089.
Values may be sent and summed in bfloat16 or wider, within the bound.
A program may use at most 192 MiB of HBM per device.

v0:
```python
import jax
import jax.numpy as jnp
from jax import lax
from jax.sharding import PartitionSpec as P


def from_behind(x, axis, by):
    length = lax.axis_size(axis)
    pairs = [(i, i + by) for i in range(length) if 0 <= i + by < length]
    return lax.ppermute(x, axis, pairs)


def normalize(rows_in, gain):
    values = rows_in.astype(jnp.float32)
    mean_square = jnp.mean(values * values, axis=-1, keepdims=True)
    return values * lax.rsqrt(mean_square + 1e-06) * gain


def short_filter(product, filter_taps):
    row_total = product.shape[0]
    reach_rows = filter_taps.shape[0] - 1
    summed = filter_taps[0] * product[reach_rows:].astype(jnp.float32)
    for i in range(1, filter_taps.shape[0]):
        summed = summed + filter_taps[i] * product[reach_rows - i : row_total - i].astype(
            jnp.float32
        )
    return summed


def build_table(filter_taps):
    tap_count = filter_taps.shape[0]
    row_index = jnp.arange(64)[:, None]
    col_index = jnp.arange(64 + tap_count - 1)[None, :]
    lag_index = row_index + tap_count - 1 - col_index
    inside = (lag_index >= 0) & (lag_index < tap_count)
    picked = jnp.take(filter_taps.T, jnp.clip(lag_index, 0, tap_count - 1), axis=1)
    return jnp.where(inside[None], picked, jnp.zeros((), filter_taps.dtype))


def long_filter(product, long_table):
    row_total = product.shape[0]
    group_count = long_table.shape[0]
    span_rows = long_table.shape[2]
    out_rows = row_total - (span_rows - 64)
    grouped = product.reshape(row_total, group_count, -1)

    def block_out(block_index):
        window_rows = lax.dynamic_slice_in_dim(grouped, block_index * 64, span_rows, 0)
        return jnp.einsum(
            "gij,jgc->igc", long_table, window_rows, preferred_element_type=jnp.float32
        )

    stacked = lax.map(block_out, jnp.arange(out_rows // 64))
    return stacked.reshape(out_rows, product.shape[1])


def apply_operator(extended, gain, feature_taps, filter_fn, reach_rows):
    scaled = normalize(extended, gain)
    row_total = extended.shape[0]
    lead_rows = feature_taps.shape[1] - 1
    streams = []
    for j in range(3):
        summed = feature_taps[j, 0] * scaled[lead_rows:]
        for i in range(1, feature_taps.shape[1]):
            summed = summed + feature_taps[j, i] * scaled[lead_rows - i : row_total - i]
        streams.append(summed)
    product = (streams[1] * streams[2]).astype(jnp.bfloat16)
    filtered = filter_fn(product)
    gate_rows = streams[0][reach_rows:]
    residual = extended[lead_rows + reach_rows :].astype(jnp.float32)
    return (residual + gate_rows * filtered).astype(jnp.bfloat16)


def on_device(tokens, norm_gain, feat_taps, se_taps, mr_taps):
    lead_rows = feat_taps.shape[3] - 1
    short_reach = se_taps.shape[1] - 1
    long_reach = mr_taps.shape[1] - 1
    rim_short = lead_rows + short_reach
    rim_long = lead_rows + long_reach
    gain_pair = norm_gain[0]
    feature_pair = feat_taps[0]
    short_taps = se_taps[0]
    long_table = build_table(mr_taps[0])
    before = from_behind(tokens[-rim_short:], ("section", "ctx"), 1)
    first_out = apply_operator(
        jnp.concatenate([before, tokens], axis=0),
        gain_pair[0],
        feature_pair[0],
        lambda p: short_filter(p, short_taps),
        short_reach,
    )
    tail_rows = from_behind(first_out[-rim_long:], ("section", "ctx"), 1)
    return apply_operator(
        jnp.concatenate([tail_rows, first_out], axis=0),
        gain_pair[1],
        feature_pair[1],
        lambda p: long_filter(p, long_table),
        long_reach,
    )


def solution(mesh):
    placed = (P(("section", "ctx"), None), P(), P(), P(), P())
    return jax.shard_map(
        on_device,
        mesh=mesh,
        in_specs=placed,
        out_specs=P(("section", "ctx"), None),
        check_vma=False,
    )
```

profile of v0, /device:TPU:1, one launch (start us, length us, event | category | flops | bytes accessed | tf_op | source)
XLA Modules:
  0.0 646.9 jit_solution(66188854466838901)
XLA Ops:
  5.0 5.9 copy.15
  15.7 50.1 %gather_fusion = bf16[12224,512]{1,0:T(8,128)(2,1)} fusion(bf16[512,128]{0,1:T(8,128)(2,1)S(1)} %bitcast.54, s32[12288]{0:T(1024)S(1)} %pad_clamp_fusion), kind=kCustom, calls=%fused_computation | custom fusion | bytes 25083648 | tf_op jit(solution)/shard_map/jit(_take)/gather | solution.py:36
  65.9 12.5 %reshape.159 = bf16[64,191,512]{2,1,0:T(8,128)(2,1)} reshape(bf16[12224,512]{1,0:T(8,128)(2,1)} %gather_fusion) | data formatting | bytes 25034752 | tf_op jit(solution)/shard_map/jit(_take)/gather | solution.py:36
  80.2 4.9 fusion.5
  85.1 5.7 fusion.6
  90.9 15.7 %multiply_convert_fusion.1 = (bf16[198,8192]{0,1:T(8,128)(2,1)S(1)}, f32[198,8192]{0,1:T(8,128)}, f32[198,8192]{0,1:T(8,128)}, f32[198,8192]{0,1:T(8,128)}) fusion(f32[8192]{0:T(1024)S(1)} %bitcast.78, f32[8192]{0:T(1024)S(1)} %bitcast.79, f32[8192]{0:T(1024)S(1)} %bitcast.80, f32[8192]{0:T(1024)} %bitcast.81, f32[8192]{0:T(1024)} %bitcast.82, ...), kind=kLoop, calls=%fused_computation.30 | loop fusion | flops 19464192 | bytes 42369024 | tf_op jit(solution)/shard_map/convert_element_type | solution.py:67
  106.5 30.4 %fusion.15 = bf16[192,8192]{0,1:T(8,128)(2,1)S(1)} fusion(f32[198,8192]{0,1:T(8,128)} %get-tuple-element.63, f32[198,8192]{0,1:T(8,128)} %get-tuple-element.64, f32[198,8192]{0,1:T(8,128)} %get-tuple-element.65, bf16[192,8192]{0,1:T(8,128)(2,1)} %copy.15, bf16[198,8192]{0,1:T(8,128)(2,1)S(1)} %get-tuple-element.62, f32[8192]{0:T(1024)S(1)} %bitcast.65, ...), kind=kLoop, calls=%fused_computation.26 | loop fusion | flops 45613056 | bytes 47513600 | tf_op jit(solution)/shard_map/convert_element_type | solution.py:71
  151.1 10.9 %select_bitcast_fusion = bf16[512,64,191]{0,2,1:T(8,128)(2,1)} fusion(bf16[64,191,512]{2,1,0:T(8,128)(2,1)} %reshape.159, pred[64,191]{1,0:T(8,128)(4,1)S(1)} %copy-done.14, pred[64,191]{1,0:T(8,128)(4,1)S(1)} %copy-done.13), kind=kLoop, calls=%fused_computation.8 | loop fusion | flops 12517376 | bytes 25059200 | tf_op jit(solution)/shard_map/jit(_where)/select_n | solution.py:37
  162.0 23.3 %copy.20 = bf16[512,64,191]{2,1,0:T(8,128)(2,1)} copy(bf16[512,64,191]{0,2,1:T(8,128)(2,1)} %select_bitcast_fusion) | data formatting | bytes 25034752 | tf_op jit(solution)/shard_map/while | solution.py:53
  185.5 18.3 %collective-permute-done.1 = bf16[129,8192]{1,0:T(8,128)(2,1)} collective-permute-done((bf16[129,8192]{1,0:T(8,128)(2,1)S(1)}, bf16[129,8192]{1,0:T(8,128)(2,1)}, u32[]{:S(2)}, u32[]{:S(2)}) %collective-permute-start.1) | collective-permute-done | bytes 2113568 | tf_op jit(solution)/shard_map/ppermute | solution.py:10
  203.8 5.6 copy.19
  209.4 6.9 %fusion.3 = f32[321]{0:T(512)S(1)} fusion(bf16[192,8192]{0,1:T(8,128)(2,1)} %copy-done.2, bf16[129,8192]{0,1:T(8,128)(2,1)} %copy.19), kind=kLoop, calls=%fused_computation.6 | loop fusion | flops 15777471 | bytes 5260548 | tf_op jit(solution)/shard_map/reduce_sum | solution.py:15
  216.4 6.7 %fusion.4 = f32[321,8192]{0,1:T(8,128)} fusion(f32[8192]{0:T(1024)S(1)} %bitcast.73, f32[321]{0:T(512)S(1)} %add_rsqrt_fusion, bf16[192,8192]{0,1:T(8,128)(2,1)S(1)} %copy-done.3, bf16[129,8192]{0,1:T(8,128)(2,1)S(1)} %copy-done.5), kind=kLoop, calls=%fused_computation.7 | loop fusion | flops 15777792 | bytes 15811844 | tf_op jit(solution)/shard_map/mul | solution.py:16
  223.1 27.4 %fusion.23 = (f32[319,8192]{0,1:T(8,128)}, bf16[319,8192]{0,1:T(8,128)(2,1)}, f32[319,8192]{0,1:T(8,128)}, f32[319,8192]{0,1:T(8,128)}) fusion(f32[321,8192]{0,1:T(8,128)} %fusion.4, f32[8192]{0:T(1024)S(1)} %bitcast.67, f32[8192]{0:T(1024)S(1)} %bitcast.68, f32[8192]{0:T(1024)S(1)} %bitcast.69, f32[8192]{0:T(1024)S(1)} %bitcast.70, f32[8192]{0:T(1024)S(1)} %bitcast.71, ...), kind=kLoop, calls=%fused_computation.48 | loop fusion | flops 31358976 | bytes 68141056 | tf_op jit(solution)/shard_map/slice | solution.py:63
  250.5 351.6 %while.10 = (s32[]{:T(128)}, f32[3,64,512,16]{1,0,3,2:T(4,128)}, s32[3]{0:T(128)S(1)}, bf16[319,512,16]{0,2,1:T(8,128)(2,1)}, bf16[512,64,191]{2,1,0:T(8,128)(2,...) while((s32[]{:T(128)}, f32[3,64,512,16]{1,0,3,2:T(4,128)}, s32[3]{0:T(128)S(1)}, ...), condition=%wide.region_3.4_spmd, body=%wide.region_2.3_spmd.sunk | while | flops 200278016 | bytes 27263136 | solution.py:53
  251.9 11.3 %fusion.35 = f32[512,16,64]{2,1,0:T(8,128)} fusion(bf16[512,64,191]{2,1,0:T(8,128)(2,1)} %get-tuple-element.152, bf16[319,512,16]{0,2,1:T(8,128)(2,1)} %get-tuple-element.151, s32[]{:T(128)S(6)} %select_n.46), kind=kOutput, calls=%fused_computation.1.clone.1 | convolution fusion | flops 200278016 | bytes 23068676 | tf_op jit(solution)/shard_map/while/body/eval_jaxpr/gij,jgc->igc/dot_general | solution.py:49
  263.2 104.7 %dynamic_update_slice.5 = f32[3,64,512,16]{1,0,3,2:T(4,128)} dynamic-update-slice(f32[3,64,512,16]{1,0,3,2:T(4,128)} %get-tuple-element.140, f32[1,64,512,16]{1,0,3,2:T(1,128)} %bitcast.55, s32[]{:T(128)} %get-tuple-element.139, s32[]{:T(128)} %constant.26.clone.1..sunk, s32[]{:T(128)} %constant.26.clone.1..sunk, s32[]{:T(128)} %constant.26.clone.1..sunk) | dynamic-update-slice | bytes 4194308 | tf_op jit(solution)/shard_map/while/body/jit(dynamic_update_index_in_dim)/dynamic_update_slice | solution.py:53
  369.3 11.3 %fusion.35 = f32[512,16,64]{2,1,0:T(8,128)} fusion(bf16[512,64,191]{2,1,0:T(8,128)(2,1)} %get-tuple-element.152, bf16[319,512,16]{0,2,1:T(8,128)(2,1)} %get-tuple-element.151, s32[]{:T(128)S(6)} %select_n.46), kind=kOutput, calls=%fused_computation.1.clone.1 | convolution fusion | flops 200278016 | bytes 23068676 | tf_op jit(solution)/shard_map/while/body/eval_jaxpr/gij,jgc->igc/dot_general | solution.py:49
  380.6 104.7 %dynamic_update_slice.5 = f32[3,64,512,16]{1,0,3,2:T(4,128)} dynamic-update-slice(f32[3,64,512,16]{1,0,3,2:T(4,128)} %get-tuple-element.140, f32[1,64,512,16]{1,0,3,2:T(1,128)} %bitcast.55, s32[]{:T(128)} %get-tuple-element.139, s32[]{:T(128)} %constant.26.clone.1..sunk, s32[]{:T(128)} %constant.26.clone.1..sunk, s32[]{:T(128)} %constant.26.clone.1..sunk) | dynamic-update-slice | bytes 4194308 | tf_op jit(solution)/shard_map/while/body/jit(dynamic_update_index_in_dim)/dynamic_update_slice | solution.py:53
  486.7 10.7 %fusion.35 = f32[512,16,64]{2,1,0:T(8,128)} fusion(bf16[512,64,191]{2,1,0:T(8,128)(2,1)} %get-tuple-element.152, bf16[319,512,16]{0,2,1:T(8,128)(2,1)} %get-tuple-element.151, s32[]{:T(128)S(6)} %select_n.46), kind=kOutput, calls=%fused_computation.1.clone.1 | convolution fusion | flops 200278016 | bytes 23068676 | tf_op jit(solution)/shard_map/while/body/eval_jaxpr/gij,jgc->igc/dot_general | solution.py:49
  497.4 104.7 %dynamic_update_slice.5 = f32[3,64,512,16]{1,0,3,2:T(4,128)} dynamic-update-slice(f32[3,64,512,16]{1,0,3,2:T(4,128)} %get-tuple-element.140, f32[1,64,512,16]{1,0,3,2:T(1,128)} %bitcast.55, s32[]{:T(128)} %get-tuple-element.139, s32[]{:T(128)} %constant.26.clone.1..sunk, s32[]{:T(128)} %constant.26.clone.1..sunk, s32[]{:T(128)} %constant.26.clone.1..sunk) | dynamic-update-slice | bytes 4194308 | tf_op jit(solution)/shard_map/while/body/jit(dynamic_update_index_in_dim)/dynamic_update_slice | solution.py:53
  602.1 18.9 %reshape.153 = f32[192,8192]{0,1:T(8,128)} reshape(f32[3,64,512,16]{1,0,3,2:T(4,128)} %get-tuple-element.32) | data formatting | bytes 12582912 | tf_op jit(solution)/shard_map/reshape | solution.py:54
  620.9 20.0 %fusion.10 = bf16[192,8192]{0,1:T(8,128)(2,1)} fusion(f32[192,8192]{0,1:T(8,128)} %reshape.153, f32[319,8192]{0,1:T(8,128)} %get-tuple-element.60, f32[319,8192]{0,1:T(8,128)} %get-tuple-element.61, f32[319,8192]{0,1:T(8,128)} %get-tuple-element.58, bf16[192,8192]{0,1:T(8,128)(2,1)} %copy-done.2, f32[8192]{0:T(1024)S(1)} %bitcast.76, f32[8192]{0:T(1024)S(1)} %bitcast.77, ...), kind=kLoop, calls=%fused_computation.18 | loop fusion | flops 14155776 | bytes 31555584 | tf_op jit(solution)/shard_map/convert_element_type | solution.py:71
  640.9 6.0 copy.22
  (57 shorter events, 27.9 us)
Async XLA Ops:
  0.0 15.7 %copy-start = (bf16[1,128,512]{2,1,0:T(8,128)(2,1)S(1)}, bf16[1,128,512]{2,1,0:T(8,128)(2,1)}, u32[]{:S(2)}) copy-start(bf16[1,128,512]{2,1,0:T(8,128)(2,1)} %param.11) | copy-start | bytes 393220
  0.0 14.7 %copy-start.15 = (f32[1,2,8192]{2,1,0:T(2,128)S(1)}, f32[1,2,8192]{2,1,0:T(2,128)}, u32[]{:S(2)}) copy-start(f32[1,2,8192]{2,1,0:T(2,128)} %param.8) | copy-start | bytes 196612
  0.0 15.4 %copy-start.8 = (f32[1,7,8192]{2,0,1:T(1,128)S(1)}, f32[1,7,8192]{2,0,1:T(1,128)}, u32[]{:S(2)}) copy-start(f32[1,7,8192]{2,0,1:T(1,128)} %param.10) | copy-start | bytes 688132
  1.0 78.2 %collective-permute-start = (bf16[8,8192]{1,0:T(8,128)(2,1)S(1)}, bf16[8,8192]{1,0:T(8,128)(2,1)S(1)}, u32[]{:S(2)}, u32[]{:S(2)}) collective-permute-start(bf16[8,8192]{1,0:T(8,128)(2,1)S(1)} %slice.163), channel_id=1, source_target_pairs={{0,1},{1,2},{2,3},{3,4},{4,5},{5,6},{6,7},{7,8},{8,9},{9,10},{10,1... | collective-permute-start | bytes 393224 | tf_op jit(solution)/shard_map/ppermute | solution.py:10
  78.4 6.7 %copy-start.9 = (f32[1,1,8192]{2,1,0:T(1,128)S(1)}, f32[1,1,8192]{2,1,0:T(1,128)}, u32[]{:S(2)}) copy-start(f32[1,1,8192]{2,1,0:T(1,128)} %get-tuple-element.93) | copy-start | bytes 98308
  80.2 4.9 copy-start.6
  80.2 5.0 copy-start.4
  85.1 5.8 copy-start.10
  85.1 5.8 copy-start.11
  85.1 5.8 copy-start.12
  136.9 2.0 copy-start.2
  138.9 12.2 %copy-start.13 = (pred[64,191]{1,0:T(8,128)(4,1)S(1)}, pred[64,191]{1,0:T(8,128)(4,1)}, u32[]{:S(2)}) copy-start(pred[64,191]{1,0:T(8,128)(4,1)} %get-tuple-element.95) | copy-start | bytes 36676
  138.9 12.2 %copy-start.14 = (pred[64,191]{1,0:T(8,128)(4,1)S(1)}, pred[64,191]{1,0:T(8,128)(4,1)}, u32[]{:S(2)}) copy-start(pred[64,191]{1,0:T(8,128)(4,1)} %get-tuple-element.96) | copy-start | bytes 36676
  147.8 56.1 %collective-permute-start.1 = (bf16[129,8192]{1,0:T(8,128)(2,1)S(1)}, bf16[129,8192]{1,0:T(8,128)(2,1)}, u32[]{:S(2)}, u32[]{:S(2)}) collective-permute-start(bf16[129,8192]{1,0:T(8,128)(2,1)S(1)} %copy.18), channel_id=1, source_target_pairs={{0,1},{1,2},{2,3},{3,4},{4,5},{5,6},{6,7},{7,8},{8,9},{9,10},{10,1... | collective-permute-start | bytes 6340616 | tf_op jit(solution)/shard_map/ppermute | solution.py:10
  162.0 23.3 %copy-start.7 = (f32[3,3,8192]{2,1,0:T(4,128)S(1)}, f32[3,3,8192]{2,1,0:T(4,128)}, u32[]{:S(2)}) copy-start(f32[3,3,8192]{2,1,0:T(4,128)} %get-tuple-element.97) | copy-start | bytes 884740
  209.4 6.9 %copy-start.3 = (bf16[192,8192]{0,1:T(8,128)(2,1)S(1)}, bf16[192,8192]{0,1:T(8,128)(2,1)}, u32[]{:S(2)}) copy-start(bf16[192,8192]{0,1:T(8,128)(2,1)} %copy-done.2) | copy-start | bytes 9437188
  209.4 7.0 %copy-start.5 = (bf16[129,8192]{0,1:T(8,128)(2,1)S(1)}, bf16[129,8192]{0,1:T(8,128)(2,1)}, u32[]{:S(2)}) copy-start(bf16[129,8192]{0,1:T(8,128)(2,1)} %copy.19) | copy-start | bytes 6340612
  620.9 26.0 %copy-start.1 = (bf16[1,128,512]{2,1,0:T(8,128)(2,1)S(1)}, bf16[1,128,512]{2,1,0:T(8,128)(2,1)}, u32[]{:S(2)}) copy-start(bf16[1,128,512]{2,1,0:T(8,128)(2,1)} %param.11) | copy-start | bytes 393220
where the time goes:
time: 657 us; the launch traced here: 647 us
  local copies, waits for them, and re-layouts  456 us (69%)
  other arithmetic  129 us (20%)
  matrix products  33.4 us (5%)
  waiting for transfers between devices  18.3 us (3%)
  starting transfers between devices  7.3 us (1%)
    dynamic_update_slice x3, local copies, waits for them, and re-layouts, long_filter(): stacked = lax.map(block_out, jnp.arange(out_rows // 64))  314 us
    gather x2, local copies, waits for them, and re-layouts, build_table(): jnp.take(filter_taps.T, jnp.clip(lag_index, 0, tap_count - 1), axis=1)  62.7 us
    convert_element_type x2, other arithmetic, apply_operator(): return (residual + gate_rows * filtered).astype(jnp.bfloat16)  50.4 us
    dot_general x3, matrix products, block_out(): jnp.einsum('gij,jgc->igc', long_table, window_rows, preferred_element_typ...  33.4 us
    slice x1, other arithmetic, apply_operator(): summed = feature_taps[j, 0] * scaled[lead_rows:]  27.4 us
    while x1, local copies, waits for them, and re-layouts, long_filter(): stacked = lax.map(block_out, jnp.arange(out_rows // 64))  23.3 us
    reshape x1, local copies, waits for them, and re-layouts, long_filter(): return stacked.reshape(out_rows, product.shape[1])  18.9 us
    ppermute x2, waiting for transfers between devices, from_behind(): return lax.ppermute(x, axis, pairs)  18.3 us
  transfers between devices with their start and end apart: 2, of which 1 were waited for; matrix products, arithmetic and copies ran while one was open for 17% of the time, Pallas kernels for 0%

commit v1 on v0

v1 whole, which is shorter than its diff:
```python
import functools

import jax
import jax.numpy as jnp
from jax import lax
from jax.experimental import pallas as pl
from jax.experimental.pallas import tpu as pltpu
from jax.sharding import PartitionSpec as P

F32 = jnp.float32
BF16 = jnp.bfloat16
LANES = 128
WIDE = 256
CHUNKS = 4


def from_behind(x, axis, by):
    length = lax.axis_size(axis)
    pairs = [(i, i + by) for i in range(length) if 0 <= i + by < length]
    return lax.ppermute(x, axis, pairs)


def lanes_of(c, width=LANES):
    return pl.ds(pl.multiple_of(c * width, width), width)


def write_scale(total, scale_ref, channels):
    mean = jnp.sum(total, axis=-1, keepdims=True) * (1.0 / channels)
    scale_ref[...] = jnp.broadcast_to(lax.rsqrt(mean + 1e-06), scale_ref.shape)


def square_sums(x_ref, blocks):
    def add(c, total):
        v = x_ref[:, lanes_of(c)].astype(F32)
        return total + v * v

    return lax.fori_loop(0, blocks, add, jnp.zeros((x_ref.shape[0], LANES), F32))


def stream(z_ref, taps, rows):
    feat = taps.shape[0]
    total = taps[0:1] * z_ref[8 : 8 + rows]
    for i in range(1, feat):
        total = total + taps[i : i + 1] * z_ref[8 - i : 8 - i + rows]
    return total


def short_block(c, x_ref, scale_ref, z_ref, w_ref, gain_ref, feat_ref, taps_ref):
    rows = x_ref.shape[0]
    cs = lanes_of(c)
    x = x_ref[:, cs].astype(F32)
    z_ref[8:] = x * scale_ref[...] * gain_ref[:, cs]
    u1 = stream(z_ref, feat_ref[1, :, cs], rows)
    u2 = stream(z_ref, feat_ref[2, :, cs], rows)
    w_ref[8:] = (u1 * u2).astype(BF16).astype(F32)
    f = stream(w_ref, taps_ref[:, cs], rows)
    return x + stream(z_ref, feat_ref[0, :, cs], rows) * f


def tail_kernel(x_ref, gain1_ref, feat1_ref, taps_ref, gain2_ref, feat2_ref, out_ref,
                h_ref, s1_ref, s2_ref, z_ref, w_ref, z2_ref, sum_ref):
    rows, channels = x_ref.shape
    blocks = channels // LANES
    z_ref[...] = jnp.zeros_like(z_ref)
    w_ref[...] = jnp.zeros_like(w_ref)
    sum_ref[...] = jnp.zeros_like(sum_ref)
    write_scale(square_sums(x_ref, blocks), s1_ref, channels)

    @pl.loop(0, blocks)
    def _(c):
        h = short_block(c, x_ref, s1_ref, z_ref, w_ref, gain1_ref, feat1_ref, taps_ref)
        h = h.astype(BF16)
        h_ref[:, lanes_of(c)] = h
        hf = h.astype(F32)
        sum_ref[...] += hf * hf

    write_scale(sum_ref[...], s2_ref, channels)
    sent = out_ref.shape[0]

    @pl.loop(0, blocks)
    def _(c):
        cs = lanes_of(c)
        z2_ref[8:] = h_ref[:, cs].astype(F32) * s2_ref[...] * gain2_ref[:, cs]
        first = rows - sent
        u1 = stream(z2_ref.at[first:], feat2_ref[1, :, cs], sent)
        u2 = stream(z2_ref.at[first:], feat2_ref[2, :, cs], sent)
        out_ref[:, cs] = (u1 * u2).astype(BF16)


def local_kernel(lead_ref, x_ref, gain1_ref, feat1_ref, taps_ref, gain2_ref, feat2_ref,
                 h_out, u_out, w_out, x_all, h_ref, s1_ref, s2_ref, z_ref, w_ref, z2_ref, sum_ref):
    lead = lead_ref.shape[0]
    rows, channels = x_all.shape
    blocks = channels // LANES
    x_all[:lead] = lead_ref[...]
    x_all[lead:] = x_ref[...]
    z_ref[...] = jnp.zeros_like(z_ref)
    w_ref[...] = jnp.zeros_like(w_ref)
    sum_ref[...] = jnp.zeros_like(sum_ref)
    write_scale(square_sums(x_all, blocks), s1_ref, channels)

    @pl.loop(0, blocks)
    def _(c):
        h = short_block(c, x_all, s1_ref, z_ref, w_ref, gain1_ref, feat1_ref, taps_ref)
        h = h.astype(BF16)
        h_ref[:, lanes_of(c)] = h
        h_out[:, lanes_of(c)] = h[lead:]
        hf = h.astype(F32)
        sum_ref[...] += hf * hf

    write_scale(sum_ref[...], s2_ref, channels)
    kept = rows - lead

    @pl.loop(0, blocks)
    def _(c):
        cs = lanes_of(c)
        z2_ref[8:] = h_ref[:, cs].astype(F32) * s2_ref[...] * gain2_ref[:, cs]
        z = z2_ref.at[lead:]
        u1 = stream(z, feat2_ref[1, :, cs], kept)
        u2 = stream(z, feat2_ref[2, :, cs], kept)
        w_out[:, cs] = (u1 * u2).astype(BF16)
        u_out[:, cs] = stream(z, feat2_ref[0, :, cs], kept)


def long_kernel(tap_count, per_group, base_ref, halo_ref, w_ref, u_ref, h_ref, *rest):
    out_ref, table, window = rest[-3:]
    kept, width = w_ref.shape
    groups = width // per_group
    for g in range(groups):
        row = jnp.broadcast_to(base_ref[g : g + 1, :], (tap_count, 2 * tap_count))
        rolled = pltpu.roll(row, 0, 1, stride=1, stride_axis=0)
        table[g * tap_count : (g + 1) * tap_count] = rolled.astype(BF16)
    lane_group = lax.broadcasted_iota(jnp.int32, (tap_count, width), 1) // per_group
    window[:tap_count] = halo_ref[...]
    window[tap_count : tap_count + kept] = w_ref[...]
    window[tap_count + kept :] = jnp.zeros((window.shape[0] - tap_count - kept, width), BF16)
    start = 0
    while start < kept:
        count = min(tap_count, kept - start)
        product = jnp.dot(table[...], window[start : start + 2 * tap_count],
                          preferred_element_type=F32)
        f = product[0:count]
        for g in range(1, groups):
            f = jnp.where(lane_group[:count] == g,
                          product[g * tap_count : g * tap_count + count], f)
        part = slice(start, start + count)
        out_ref[part] = (h_ref[part].astype(F32) + u_ref[part] * f).astype(BF16)
        start += count


def whole():
    return pl.BlockSpec(memory_space=pltpu.VMEM)


def on_device(tokens, norm_gain, feat_taps, se_taps, mr_taps):
    rows, channels = tokens.shape
    tap_count, group_count = mr_taps.shape[1:]
    per_group = channels // group_count
    gain1, gain2 = norm_gain[0, 0:1], norm_gain[0, 1:2]
    feat1, feat2 = feat_taps[0, 0], feat_taps[0, 1]
    short = se_taps[0]
    lead = 16
    tail = tap_count + 16
    params = pltpu.CompilerParams(vmem_limit_bytes=60 * 1024 * 1024)
    before = from_behind(tokens[-lead:], ("section", "ctx"), 1)

    def scratch(count):
        return [
            pltpu.VMEM((count, channels), BF16),
            pltpu.VMEM((count, LANES), F32),
            pltpu.VMEM((count, LANES), F32),
            pltpu.VMEM((8 + count, LANES), F32),
            pltpu.VMEM((8 + count, LANES), F32),
            pltpu.VMEM((8 + count, LANES), F32),
            pltpu.VMEM((count, LANES), F32),
        ]

    sent = pl.pallas_call(
        tail_kernel,
        out_shape=jax.ShapeDtypeStruct((tap_count, channels), BF16),
        in_specs=[whole()] * 6,
        out_specs=whole(),
        scratch_shapes=scratch(tail),
        compiler_params=params,
        name="tail",
    )(tokens[-tail:], gain1, feat1, short, gain2, feat2)
    part = channels // CHUNKS
    halos = [from_behind(sent[:, k * part : (k + 1) * part], ("section", "ctx"), 1)
             for k in range(CHUNKS)]
    h, u, w = pl.pallas_call(
        local_kernel,
        out_shape=(
            jax.ShapeDtypeStruct((rows, channels), BF16),
            jax.ShapeDtypeStruct((rows, channels), F32),
            jax.ShapeDtypeStruct((rows, channels), BF16),
        ),
        in_specs=[whole()] * 7,
        out_specs=(whole(),) * 3,
        scratch_shapes=[pltpu.VMEM((rows + lead, channels), BF16)] + scratch(rows + lead),
        compiler_params=params,
        name="local",
    )(before, tokens, gain1, feat1, short, gain2, feat2)
    base = jnp.pad(mr_taps[0].astype(F32).T[:, ::-1], ((0, 0), (1, tap_count - 1)))
    out = None
    window_rows = -(-rows // tap_count) * tap_count + tap_count
    for k in range(CHUNKS):
        first = k * part // WIDE
        here = lambda i, first=first: (0, first + i)
        operands = [base, halos[k], w, u, h]
        specs = [
            pl.BlockSpec((WIDE // per_group, 2 * tap_count), lambda i, first=first: (first + i, 0)),
            pl.BlockSpec((tap_count, WIDE), lambda i: (0, i)),
            pl.BlockSpec((rows, WIDE), here),
            pl.BlockSpec((rows, WIDE), here),
            pl.BlockSpec((rows, WIDE), here),
        ]
        aliases = {}
        if out is not None:
            operands.append(out)
            specs.append(pl.BlockSpec(memory_space=pl.ANY))
            aliases = {5: 0}
        out = pl.pallas_call(
            functools.partial(long_kernel, tap_count, per_group),
            out_shape=jax.ShapeDtypeStruct((rows, channels), BF16),
            grid=(part // WIDE,),
            in_specs=specs,
            out_specs=pl.BlockSpec((rows, WIDE), here),
            scratch_shapes=[
                pltpu.VMEM((WIDE // per_group * tap_count, 2 * tap_count), BF16),
                pltpu.VMEM((window_rows, WIDE), BF16),
            ],
            input_output_aliases=aliases,
            compiler_params=params,
            name="long",
        )(*operands)
    return out


def solution(mesh):
    placed = (P(("section", "ctx"), None), P(), P(), P(), P())
    return jax.shard_map(
        on_device,
        mesh=mesh,
        in_specs=placed,
        out_specs=P(("section", "ctx"), None),
        check_vma=False,
    )
```

time: 657 us -> 158 us (0.24); the launches traced: 647 us -> 157 us
  local copies, waits for them, and re-layouts: 456 us -> 19.6 us
  other arithmetic: 129 us -> 0.02 us
  Pallas kernels: 0 us -> 78.9 us
  matrix products: 33.4 us -> 0 us
  waiting for transfers between devices: 18.3 us -> 41.3 us
  starting transfers between devices: 7.3 us -> 16.5 us
    dynamic_update_slice x3 -> x0, local copies, waits for them, and re-layouts: 314 us -> none  [long_filter(): stacked = lax.map(block_out, jnp.arange(out_rows // 64))]
    pallas_call x0 -> x6, Pallas kernels: none -> 78.9 us  [the longest x4 36 us: on_device(): pl.pallas_call(functools.partial(long_kernel, tap_count, per_group), out_...]
    convert_element_type x3 -> x0, other arithmetic: 66 us -> none  [the longest x2 50.4 us: apply_operator(): return (residual + gate_rows * filtered).astype(jnp.bfloat16)]
    gather x2 -> x0, local copies, waits for them, and re-layouts: 62.7 us -> none  [build_table(): jnp.take(filter_taps.T, jnp.clip(lag_index, 0, tap_count - 1), axis=1)]
    dot_general x3 -> x0, matrix products: 33.4 us -> none  [block_out(): jnp.einsum('gij,jgc->igc', long_table, window_rows, preferred_element_typ...]
    slice x1 -> x0, other arithmetic: 27.4 us -> none  [apply_operator(): summed = feature_taps[j, 0] * scaled[lead_rows:]]
    while x1 -> x0, local copies, waits for them, and re-layouts: 23.3 us -> none  [long_filter(): stacked = lax.map(block_out, jnp.arange(out_rows // 64))]
    ppermute x2 -> x5, waiting for transfers between devices: 18.3 us -> 41.3 us  [from_behind(): return lax.ppermute(x, axis, pairs)]
  transfers between devices with their start and end apart: 2 -> 5, of which waited for: 1 -> 1; matrix products, arithmetic and copies ran while one was open for 17% -> 2% of each run, Pallas kernels for 0% -> 35%
where the time goes in v1:
time: 158 us; the launch traced here: 157 us
  Pallas kernels  78.9 us (50%)
  waiting for transfers between devices  41.3 us (26%)
  local copies, waits for them, and re-layouts  19.6 us (12%)
  starting transfers between devices  16.5 us (10%)
    ppermute x5, waiting for transfers between devices, from_behind(): return lax.ppermute(x, axis, pairs)  41.3 us
    pallas_call x4, Pallas kernels, on_device(): pl.pallas_call(functools.partial(long_kernel, tap_count, per_group), out_...  36 us
    pallas_call x1, Pallas kernels, on_device(): pl.pallas_call(local_kernel, out_shape=(jax.ShapeDtypeStruct((rows, chann...  27.3 us
    ppermute x5, starting transfers between devices, from_behind(): return lax.ppermute(x, axis, pairs)  16.5 us
    pallas_call x1, Pallas kernels, on_device(): pl.pallas_call(tail_kernel, out_shape=jax.ShapeDtypeStruct((tap_count, ch...  15.7 us
    unnamed x14, local copies, waits for them, and re-layouts  5.81 us
    slice x1, local copies, waits for them, and re-layouts, on_device(): tokens[-tail:]  3.28 us
  transfers between devices with their start and end apart: 5, of which 1 were waited for; matrix products, arithmetic and copies ran while one was open for 2% of the time, Pallas kernels for 35%

profile of v1, /device:TPU:1, one launch (start us, length us, event | category | flops | bytes accessed | tf_op | source)
XLA Modules:
  0.0 156.6 jit_solution(15093743412440929772)
XLA Ops:
  0.0 1.6 %slice_bitcast_fusion = (f32[1,8192]{1,0:T(1,128)}, f32[1,8192]{1,0:T(1,128)}) fusion(f32[1,2,8192]{2,1,0:T(2,128)} %param.6), kind=kLoop, calls=%fused_computation.4 | loop fusion | bytes 131072 | tf_op jit(solution)/shard_map/squeeze | solution.py:159
  1.6 1.8 %copy.18 = f32[1,7,8192]{2,1,0:T(8,128)} copy(f32[1,7,8192]{2,0,1:T(1,128)} %param.8) | data formatting | bytes 458752
  3.4 1.8 %fusion.1 = (f32[1,1,3,3,8192]{4,1,3,2,0:T(1,128)S(1)}, f32[1,1,3,3,8192]{4,1,3,2,0:T(1,128)S(1)}) fusion(f32[1,2,3,3,8192]{4,1,3,2,0:T(2,128)} %param.7), kind=kLoop, calls=%fused_computation.7 | loop fusion | bytes 1179648 | tf_op jit(solution)/shard_map/slice | solution.py:160
  5.2 3.3 %slice.30.x_ref = bf16[144,8192]{1,0:T(8,128)(2,1)} slice(bf16[192,8192]{1,0:T(8,128)(2,1)} %x_ref.1), slice={[48:192], [0:8192]} | slice | bytes 4718592 | tf_op jit(solution)/shard_map/slice | solution.py:186
  8.5 1.3 copy_bitcast_fusion
  9.8 15.7 %tail.1 = bf16[128,8192]{1,0:T(8,128)(2,1)} custom-call(bf16[144,8192]{1,0:T(8,128)(2,1)} %slice.30.x_ref, f32[1,8192]{1,0:T(1,128)} %get-tuple-element.18.gain1_ref, f32[3,3,8192]{2,1,0:T(4,128)} %get-tuple-element.20.feat1_ref, f32[7,8192]{1,0:T(8,128)} %bitcast.16, f32[1,8192]{1,0:T(1,128)} %get-tuple-element.17.gain2_ref, ...), custom_call_target="tpu_custom_call" | custom-call | tf_op jit(solution)/shard_map/tail/pallas_call | solution.py:178
  25.5 2.8 %fusion = (bf16[128,2048]{1,0:T(8,128)(2,1)}, bf16[128,2048]{1,0:T(8,128)(2,1)}, bf16[128,2048]{1,0:T(8,128)(2,1)}, bf16[128,2048]{1,0:T(8,128)(2,1)S(1)}) fusion(bf16[128,8192]{1,0:T(8,128)(2,1)} %tail.1), kind=kLoop, calls=%fused_computation.6 | loop fusion | bytes 4194304 | tf_op jit(solution)/shard_map/slice | solution.py:188
  28.2 4.0 %collective-permute-start.4 = (bf16[128,2048]{1,0:T(8,128)(2,1)}, bf16[128,2048]{1,0:T(8,128)(2,1)S(1)}, u32[]{:S(2)}, u32[]{:S(2)}) collective-permute-start(bf16[128,2048]{1,0:T(8,128)(2,1)} %get-tuple-element.11), channel_id=1, source_target_pairs={{0,1},{1,2},{2,3},{3,4},{4,5},{5,6},{6,7},{7,8},{8,9},{9,10},{10,1... | collective-permute-start | bytes 1572872 | tf_op jit(solution)/shard_map/ppermute | solution.py:20
  32.2 3.1 %collective-permute-start.3 = (bf16[128,2048]{1,0:T(8,128)(2,1)}, bf16[128,2048]{1,0:T(8,128)(2,1)S(1)}, u32[]{:S(2)}, u32[]{:S(2)}) collective-permute-start(bf16[128,2048]{1,0:T(8,128)(2,1)} %get-tuple-element.12), channel_id=1, source_target_pairs={{0,1},{1,2},{2,3},{3,4},{4,5},{5,6},{6,7},{7,8},{8,9},{9,10},{10,1... | collective-permute-start | bytes 1572872 | tf_op jit(solution)/shard_map/ppermute | solution.py:20
  35.3 3.1 %collective-permute-start.2 = (bf16[128,2048]{1,0:T(8,128)(2,1)}, bf16[128,2048]{1,0:T(8,128)(2,1)S(1)}, u32[]{:S(2)}, u32[]{:S(2)}) collective-permute-start(bf16[128,2048]{1,0:T(8,128)(2,1)} %get-tuple-element.13), channel_id=1, source_target_pairs={{0,1},{1,2},{2,3},{3,4},{4,5},{5,6},{6,7},{7,8},{8,9},{9,10},{10,1... | collective-permute-start | bytes 1572872 | tf_op jit(solution)/shard_map/ppermute | solution.py:20
  38.5 3.1 %collective-permute-start = (bf16[128,2048]{1,0:T(8,128)(2,1)S(1)}, bf16[128,2048]{1,0:T(8,128)(2,1)S(1)}, u32[]{:S(2)}, u32[]{:S(2)}) collective-permute-start(bf16[128,2048]{1,0:T(8,128)(2,1)S(1)} %get-tuple-element.14), channel_id=1, source_target_pairs={{0,1},{1,2},{2,3},{3,4},{4,5},{5,6},{6,7},{7,8},{8,9},{9,10},{10,1... | collective-permute-start | bytes 1572872 | tf_op jit(solution)/shard_map/ppermute | solution.py:20
  41.7 1.7 %slice.36 = bf16[16,8192]{1,0:T(8,128)(2,1)} slice(bf16[192,8192]{1,0:T(8,128)(2,1)} %x_ref.1), slice={[176:192], [0:8192]} | slice | bytes 524288 | tf_op jit(solution)/shard_map/slice | solution.py:165
  43.3 3.1 %collective-permute-start.1 = (bf16[16,8192]{1,0:T(8,128)(2,1)}, bf16[16,8192]{1,0:T(8,128)(2,1)S(1)}, u32[]{:S(2)}, u32[]{:S(2)}) collective-permute-start(bf16[16,8192]{1,0:T(8,128)(2,1)} %slice.36), channel_id=1, source_target_pairs={{0,1},{1,2},{2,3},{3,4},{4,5},{5,6},{6,7},{7,8},{8,9},{9,10},{10,1... | collective-permute-start | bytes 786440 | tf_op jit(solution)/shard_map/ppermute | solution.py:20
  47.0 1.0 pad.4.base_ref
  48.0 41.3 %collective-permute-done.1.lead_ref = bf16[16,8192]{1,0:T(8,128)(2,1)S(1)} collective-permute-done((bf16[16,8192]{1,0:T(8,128)(2,1)}, bf16[16,8192]{1,0:T(8,128)(2,1)S(1)}, u32[]{:S(2)}, u32[]{:S(2)}) %collective-permute-start.1) | collective-permute-done | bytes 262176 | tf_op jit(solution)/shard_map/ppermute | solution.py:20
  90.1 27.3 %local.1 = (bf16[192,8192]{1,0:T(8,128)(2,1)}, f32[192,8192]{1,0:T(8,128)}, bf16[192,8192]{1,0:T(8,128)(2,1)}) custom-call(bf16[16,8192]{1,0:T(8,128)(2,1)} %copy-done.4, bf16[192,8192]{1,0:T(8,128)(2,1)} %x_ref.1, f32[1,8192]{1,0:T(1,128)} %get-tuple-element.18.gain1_ref, f32[3,3,8192]{2,1,0:T(4,128)} %get-tuple-element.20.feat1_ref, f32[7,8192]{1,0:T(8,128)} %bitcast.17, ...), custom_call_target="tpu_custom_call" | custom-call | tf_op jit(solution)/shard_map/local/pallas_call | solution.py:190
  117.4 0.8 copy-done.3
  118.2 9.0 %long.4.rest_0_ = bf16[192,8192]{1,0:T(8,128)(2,1)} custom-call(f32[512,256]{1,0:T(8,128)} %pad.4.base_ref, bf16[128,2048]{1,0:T(8,128)(2,1)} %copy-done.3, bf16[192,8192]{1,0:T(8,128)(2,1)} %get-tuple-element.8.w_ref, f32[192,8192]{1,0:T(8,128)} %get-tuple-element.9.u_ref, bf16[192,8192]{1,0:T(8,128)(2,1)} %get-tuple-element.10.h_ref), custom_call_target="tpu_custom_call" | custom-call | tf_op jit(solution)/shard_map/long/pallas_call | solution.py:222
  127.1 0.8 copy-done.2
  128.0 9.0 %long.5.rest_0_ = bf16[192,8192]{1,0:T(8,128)(2,1)} custom-call(f32[512,256]{1,0:T(8,128)} %pad.4.base_ref, bf16[128,2048]{1,0:T(8,128)(2,1)} %copy-done.2, bf16[192,8192]{1,0:T(8,128)(2,1)} %get-tuple-element.8.w_ref, f32[192,8192]{1,0:T(8,128)} %get-tuple-element.9.u_ref, ...), custom_call_target="tpu_custom_call", output_to_operand_aliasing={{}: (5, {})} | custom-call | tf_op jit(solution)/shard_map/long/pallas_call | solution.py:222
  137.0 0.8 copy-done.1
  137.8 9.0 %long.6.rest_0_ = bf16[192,8192]{1,0:T(8,128)(2,1)} custom-call(f32[512,256]{1,0:T(8,128)} %pad.4.base_ref, bf16[128,2048]{1,0:T(8,128)(2,1)} %copy-done.1, bf16[192,8192]{1,0:T(8,128)(2,1)} %get-tuple-element.8.w_ref, f32[192,8192]{1,0:T(8,128)} %get-tuple-element.9.u_ref, ...), custom_call_target="tpu_custom_call", output_to_operand_aliasing={{}: (5, {})} | custom-call | tf_op jit(solution)/shard_map/long/pallas_call | solution.py:222
  146.8 0.8 copy-done
  147.6 9.0 %long.7 = bf16[192,8192]{1,0:T(8,128)(2,1)} custom-call(f32[512,256]{1,0:T(8,128)} %pad.4.base_ref, bf16[128,2048]{1,0:T(8,128)(2,1)} %copy-done, bf16[192,8192]{1,0:T(8,128)(2,1)} %get-tuple-element.8.w_ref, f32[192,8192]{1,0:T(8,128)} %get-tuple-element.9.u_ref, bf16[192,8192]{1,0:T(8,128)(2,1)} %get-tuple-element.10.h_ref, ...), custom_call_target="tpu_custom_call", output_to_operand_aliasing={{}: (5, {})} | custom-call | tf_op jit(solution)/shard_map/long/pallas_call | solution.py:222
  (15 shorter events, 1.2 us)
Async XLA Ops:
  25.5 21.0 %copy-start.5 = (bf16[1,128,512]{2,1,0:T(8,128)(2,1)S(1)}, bf16[1,128,512]{2,1,0:T(8,128)(2,1)}, u32[]{:S(2)}) copy-start(bf16[1,128,512]{2,1,0:T(8,128)(2,1)} %param.9) | copy-start | bytes 393220
  28.2 89.1 %collective-permute-start.4 = (bf16[128,2048]{1,0:T(8,128)(2,1)}, bf16[128,2048]{1,0:T(8,128)(2,1)S(1)}, u32[]{:S(2)}, u32[]{:S(2)}) collective-permute-start(bf16[128,2048]{1,0:T(8,128)(2,1)} %get-tuple-element.11), channel_id=1, source_target_pairs={{0,1},{1,2},{2,3},{3,4},{4,5},{5,6},{6,7},{7,8},{8,9},{9,10},{10,1... | collective-permute-start | bytes 1572872 | tf_op jit(solution)/shard_map/ppermute | solution.py:20
  32.2 94.9 %collective-permute-start.3 = (bf16[128,2048]{1,0:T(8,128)(2,1)}, bf16[128,2048]{1,0:T(8,128)(2,1)S(1)}, u32[]{:S(2)}, u32[]{:S(2)}) collective-permute-start(bf16[128,2048]{1,0:T(8,128)(2,1)} %get-tuple-element.12), channel_id=1, source_target_pairs={{0,1},{1,2},{2,3},{3,4},{4,5},{5,6},{6,7},{7,8},{8,9},{9,10},{10,1... | collective-permute-start | bytes 1572872 | tf_op jit(solution)/shard_map/ppermute | solution.py:20
  35.3 101.6 %collective-permute-start.2 = (bf16[128,2048]{1,0:T(8,128)(2,1)}, bf16[128,2048]{1,0:T(8,128)(2,1)S(1)}, u32[]{:S(2)}, u32[]{:S(2)}) collective-permute-start(bf16[128,2048]{1,0:T(8,128)(2,1)} %get-tuple-element.13), channel_id=1, source_target_pairs={{0,1},{1,2},{2,3},{3,4},{4,5},{5,6},{6,7},{7,8},{8,9},{9,10},{10,1... | collective-permute-start | bytes 1572872 | tf_op jit(solution)/shard_map/ppermute | solution.py:20
  38.5 108.2 %collective-permute-start = (bf16[128,2048]{1,0:T(8,128)(2,1)S(1)}, bf16[128,2048]{1,0:T(8,128)(2,1)S(1)}, u32[]{:S(2)}, u32[]{:S(2)}) collective-permute-start(bf16[128,2048]{1,0:T(8,128)(2,1)S(1)} %get-tuple-element.14), channel_id=1, source_target_pairs={{0,1},{1,2},{2,3},{3,4},{4,5},{5,6},{6,7},{7,8},{8,9},{9,10},{10,1... | collective-permute-start | bytes 1572872 | tf_op jit(solution)/shard_map/ppermute | solution.py:20
  43.3 46.0 %collective-permute-start.1 = (bf16[16,8192]{1,0:T(8,128)(2,1)}, bf16[16,8192]{1,0:T(8,128)(2,1)S(1)}, u32[]{:S(2)}, u32[]{:S(2)}) collective-permute-start(bf16[16,8192]{1,0:T(8,128)(2,1)} %slice.36), channel_id=1, source_target_pairs={{0,1},{1,2},{2,3},{3,4},{4,5},{5,6},{6,7},{7,8},{8,9},{9,10},{10,1... | collective-permute-start | bytes 786440 | tf_op jit(solution)/shard_map/ppermute | solution.py:20
  89.4 0.7 copy-start.4
  117.4 0.8 copy-start.3
  127.1 0.8 copy-start.2
  137.0 0.8 copy-start.1
  146.8 0.8 copy-start

commit v2 on v0

v2 whole, which is shorter than its diff:
```python
import functools

import jax
import jax.numpy as jnp
from jax import lax
from jax.experimental import pallas as pl
from jax.experimental.pallas import tpu as pltpu
from jax.sharding import PartitionSpec as P

F32 = jnp.float32
BF16 = jnp.bfloat16
LANES = 128
CHUNKS = 8
LEAD = 16
MESH = pl.DeviceIdType.MESH


def lanes_of(c, width=LANES):
    return pl.ds(pl.multiple_of(c * width, width), width)


def row_scale(total, channels):
    mean = jnp.sum(total, axis=-1, keepdims=True) * (1.0 / channels)
    return jnp.broadcast_to(lax.rsqrt(mean + 1e-06), total.shape)


def square_sums(read, rows, blocks):
    def add(c, total):
        v = read(c).astype(F32)
        return total + v * v

    return lax.fori_loop(0, blocks, add, jnp.zeros((rows, LANES), F32))


def stream(z_ref, taps, first, rows):
    total = taps[0:1] * z_ref[8 + first : 8 + first + rows]
    for i in range(1, taps.shape[0]):
        total = total + taps[i : i + 1] * z_ref[8 + first - i : 8 + first - i + rows]
    return total


def pieces(rows, most=48):
    return [(first, min(most, rows - first)) for first in range(0, rows, most)]


def short_rows(read, rows, start, blocks, channels, gain_ref, feat_ref, taps_ref, h_ref,
               scale_ref, z_ref, w_ref, s_ref, sum_ref):
    s_ref[:rows] = row_scale(square_sums(read, rows, blocks), channels)
    sum_ref[:rows] = jnp.zeros((rows, LANES), F32)

    @pl.loop(0, blocks)
    def _(c):
        cs = lanes_of(c)
        gain = gain_ref[0, 0:1, cs]
        taps = [feat_ref[0, 0, j, :, cs] * gain for j in range(3)]
        short = taps_ref[0, :, cs]
        z_ref[8 : 8 + rows] = read(c).astype(F32) * s_ref[:rows]
        for first, count in pieces(rows):
            u1 = stream(z_ref, taps[1], first, count)
            u2 = stream(z_ref, taps[2], first, count)
            w_ref[8 + first : 8 + first + count] = (u1 * u2).astype(BF16).astype(F32)
        for first, count in pieces(rows):
            f = stream(w_ref, short, first, count)
            u0 = stream(z_ref, taps[0], first, count)
            h_ref[start + first : start + first + count, cs] = u0 * f
        h = (h_ref[start : start + rows, cs] + read(c).astype(F32)).astype(BF16).astype(F32)
        h_ref[start : start + rows, cs] = h
        sum_ref[:rows] += h * h

    scale_ref[start : start + rows] = row_scale(sum_ref[:rows], channels)


def kernel(axes, x_ref, gain_ref, feat_ref, taps_ref, mr_ref, out_ref,
           lead_ref, win_ref, h_ref, u_ref, table_ref, base_ref, rhs_ref, scale_ref, z_ref, w_ref,
           s_ref, sum_ref, lead_sems, send_sems, recv_sems):
    rows, channels = x_ref.shape
    tap_count, group_count = mr_ref.shape[1:]
    per_group = channels // group_count
    groups = LANES // per_group
    half = rows // 2
    blocks = channels // LANES
    part = channels // CHUNKS
    outer, inner = axes
    inner_size = lax.axis_size(inner)
    count = lax.axis_size(outer) * inner_size
    me = lax.axis_index(outer) * inner_size + lax.axis_index(inner)
    behind, ahead = me - 1, me + 1
    has_behind, has_ahead = me > 0, me < count - 1

    def place(index):
        return (index // inner_size, index % inner_size)

    barrier = pltpu.get_barrier_semaphore()

    @pl.when(has_behind)
    def _():
        pl.semaphore_signal(barrier, inc=1, device_id=place(behind), device_id_type=MESH)

    @pl.when(has_ahead)
    def _():
        pl.semaphore_signal(barrier, inc=1, device_id=place(ahead), device_id_type=MESH)

    peers = has_behind.astype(jnp.int32) + has_ahead.astype(jnp.int32)
    pl.semaphore_wait(barrier, peers)

    def lead_copy():
        return pltpu.make_async_remote_copy(
            src_ref=x_ref.at[pl.ds(rows - LEAD, LEAD)], dst_ref=lead_ref,
            send_sem=lead_sems.at[0], recv_sem=lead_sems.at[1],
            device_id=place(ahead), device_id_type=MESH)

    def part_copy(k):
        cs = lanes_of(k, part)
        return pltpu.make_async_remote_copy(
            src_ref=win_ref.at[pl.ds(rows, tap_count), cs],
            dst_ref=win_ref.at[pl.ds(0, tap_count), cs],
            send_sem=send_sems.at[k], recv_sem=recv_sems.at[k],
            device_id=place(ahead), device_id_type=MESH)

    @pl.when(has_ahead)
    def _():
        lead_copy().start()

    z_ref[...] = jnp.zeros_like(z_ref)
    w_ref[...] = jnp.zeros_like(w_ref)
    share = (blocks, channels, gain_ref, feat_ref, taps_ref, h_ref, scale_ref, z_ref, w_ref,
             s_ref, sum_ref)

    tail = tap_count + LEAD
    first_tail = rows - tail
    short_rows(lambda c: x_ref[first_tail:, lanes_of(c)], tail, LEAD + first_tail, *share)
    first_sent = rows - tap_count

    @pl.loop(0, CHUNKS)
    def _(k):
        @pl.loop(0, blocks // CHUNKS)
        def _(b):
            cs = lanes_of(k * (blocks // CHUNKS) + b)
            gain = gain_ref[0, 1:2, cs]
            taps = [feat_ref[0, 1, j, :, cs] * gain for j in range(3)]
            n = tap_count + 8
            top = LEAD + first_sent - 8
            z_ref[0:n] = h_ref[top : top + n, cs] * scale_ref[top : top + n]
            for first, size in pieces(tap_count):
                u1 = stream(z_ref, taps[1], first, size)
                u2 = stream(z_ref, taps[2], first, size)
                win_ref[rows + first : rows + first + size, cs] = (u1 * u2).astype(BF16)

        @pl.when(has_ahead & (k > 0))
        def _():
            part_copy(k - 1).start()

    spread = 2 * tap_count
    at_tap = lax.broadcasted_iota(jnp.int32, (tap_count, spread), 0)
    at_lag = lax.broadcasted_iota(jnp.int32, (tap_count, spread), 1)
    flip = jnp.where(at_tap + at_lag == tap_count, 1.0, 0.0).astype(BF16)
    base_ref[...] = lax.dot_general(mr_ref[0], flip, (((0,), (0,)), ((), ())),
                                    preferred_element_type=F32)
    rhs_ref[...] = jnp.zeros_like(rhs_ref)

    @pl.when(has_ahead)
    def _():
        part_copy(CHUNKS - 1).start()

    @pl.when(has_behind)
    def _():
        lead_copy().wait_recv()

    @pl.when(jnp.logical_not(has_behind))
    def _():
        lead_ref[...] = jnp.zeros_like(lead_ref)
        win_ref[:tap_count] = jnp.zeros((tap_count, channels), BF16)

    head = LEAD + first_sent
    z_ref[0:8] = jnp.zeros((8, LANES), F32)
    short_rows(
        lambda c: jnp.concatenate([lead_ref[:, lanes_of(c)], x_ref[:first_sent, lanes_of(c)]], axis=0),
        head, 0, *share)

    @pl.loop(0, blocks)
    def _(c):
        cs = lanes_of(c)
        gain = gain_ref[0, 1:2, cs]
        taps = [feat_ref[0, 1, j, :, cs] * gain for j in range(3)]
        z_ref[0 : rows + 8] = h_ref[LEAD - 8 :, cs] * scale_ref[LEAD - 8 :]
        for first, size in pieces(first_sent):
            u1 = stream(z_ref, taps[1], first, size)
            u2 = stream(z_ref, taps[2], first, size)
            win_ref[tap_count + first : tap_count + first + size, cs] = (u1 * u2).astype(BF16)
        for first, size in pieces(rows):
            u_ref[first : first + size, cs] = stream(z_ref, taps[0], first, size)

    @pl.loop(0, blocks)
    def _(c):
        lags = base_ref[pl.ds(pl.multiple_of(c * groups, groups), groups), :]
        for g in range(groups):
            row = jnp.broadcast_to(lags[g : g + 1], (half, spread))
            rolled = pltpu.roll(row, 0, 1, stride=1, stride_axis=0)
            table_ref[c, g * half : (g + 1) * half] = rolled.astype(BF16)

    lane_group = lax.broadcasted_iota(jnp.int32, (half, LANES), 1) // per_group
    reach = half + tap_count

    @pl.loop(0, CHUNKS)
    def _(k):
        @pl.when(has_behind)
        def _():
            part_copy(k).wait_recv()

        @pl.loop(0, blocks // CHUNKS)
        def _(b):
            c = k * (blocks // CHUNKS) + b
            cs = lanes_of(c)
            rhs_ref[:reach, :LANES] = win_ref[:reach, cs]
            rhs_ref[:reach, LANES:] = win_ref[half : half + reach, cs]
            product = jnp.dot(table_ref[c], rhs_ref[...], preferred_element_type=F32)
            for side in range(2):
                ls = slice(side * LANES, (side + 1) * LANES)
                f = product[0:half, ls]
                for g in range(1, groups):
                    f = jnp.where(lane_group == g, product[g * half : (g + 1) * half, ls], f)
                rs = slice(side * half, (side + 1) * half)
                hs = slice(LEAD + side * half, LEAD + (side + 1) * half)
                out_ref[rs, cs] = (h_ref[hs, cs] + u_ref[rs, cs] * f).astype(BF16)

    @pl.when(has_ahead)
    def _():
        lead_copy().wait_send()

        @pl.loop(0, CHUNKS)
        def _(k):
            part_copy(k).wait_send()


def on_device(axes, tokens, norm_gain, feat_taps, se_taps, mr_taps):
    rows, channels = tokens.shape
    tap_count, group_count = mr_taps.shape[1:]
    groups = LANES * group_count // channels
    blocks = channels // LANES
    spread = 2 * tap_count
    return pl.pallas_call(
        functools.partial(kernel, axes),
        out_shape=jax.ShapeDtypeStruct((rows, channels), BF16),
        in_specs=[pl.BlockSpec(memory_space=pltpu.VMEM)] * 5,
        out_specs=pl.BlockSpec(memory_space=pltpu.VMEM),
        scratch_shapes=[
            pltpu.VMEM((LEAD, channels), BF16),
            pltpu.VMEM((tap_count + rows, channels), BF16),
            pltpu.VMEM((LEAD + rows, channels), F32),
            pltpu.VMEM((rows, channels), F32),
            pltpu.VMEM((blocks, groups * rows // 2, spread), BF16),
            pltpu.VMEM((group_count, spread), F32),
            pltpu.VMEM((spread, 2 * LANES), BF16),
            pltpu.VMEM((LEAD + rows, LANES), F32),
            pltpu.VMEM((LEAD + rows, LANES), F32),
            pltpu.VMEM((LEAD + rows, LANES), F32),
            pltpu.VMEM((LEAD + rows, LANES), F32),
            pltpu.VMEM((LEAD + rows, LANES), F32),
            pltpu.SemaphoreType.DMA((2,)),
            pltpu.SemaphoreType.DMA((CHUNKS,)),
            pltpu.SemaphoreType.DMA((CHUNKS,)),
        ],
        compiler_params=pltpu.CompilerParams(
            collective_id=0, has_side_effects=True, vmem_limit_bytes=67043328),
        name="pair",
    )(tokens, norm_gain, feat_taps, se_taps, mr_taps)


def solution(mesh):
    axes = tuple(mesh.axis_names)
    placed = (P(axes, None), P(), P(), P(), P())
    return jax.shard_map(
        functools.partial(on_device, axes),
        mesh=mesh,
        in_specs=placed,
        out_specs=P(axes, None),
        check_vma=False,
    )
```

time: 657 us -> 78.1 us (0.12); the launches traced: 647 us -> 77.9 us
  local copies, waits for them, and re-layouts: 456 us -> 8 us
  other arithmetic: 129 us -> 0 us
  Pallas kernels: 0 us -> 69.9 us
  matrix products: 33.4 us -> 0 us
  waiting for transfers between devices: 18.3 us -> 0 us
  starting transfers between devices: 7.3 us -> 0 us
    dynamic_update_slice x3 -> x0, local copies, waits for them, and re-layouts: 314 us -> none  [long_filter(): stacked = lax.map(block_out, jnp.arange(out_rows // 64))]
    pallas_call x0 -> x1, Pallas kernels: none -> 69.9 us  [on_device(): pl.pallas_call(functools.partial(kernel, axes), out_shape=jax.ShapeDtypeS...]
    convert_element_type x3 -> x0, other arithmetic: 66 us -> none  [the longest x2 50.4 us: apply_operator(): return (residual + gate_rows * filtered).astype(jnp.bfloat16)]
    gather x2 -> x0, local copies, waits for them, and re-layouts: 62.7 us -> none  [build_table(): jnp.take(filter_taps.T, jnp.clip(lag_index, 0, tap_count - 1), axis=1)]
    dot_general x3 -> x0, matrix products: 33.4 us -> none  [block_out(): jnp.einsum('gij,jgc->igc', long_table, window_rows, preferred_element_typ...]
    slice x1 -> x0, other arithmetic: 27.4 us -> none  [apply_operator(): summed = feature_taps[j, 0] * scaled[lead_rows:]]
    while x1 -> x0, local copies, waits for them, and re-layouts: 23.3 us -> none  [long_filter(): stacked = lax.map(block_out, jnp.arange(out_rows // 64))]
    reshape x1 -> x0, local copies, waits for them, and re-layouts: 18.9 us -> none  [long_filter(): return stacked.reshape(out_rows, product.shape[1])]
  transfers between devices with their start and end apart: 2 -> 0, of which waited for: 1 -> 0; matrix products, arithmetic and copies ran while one was open for 17% -> 0% of each run, Pallas kernels for 0% -> 0%
where the time goes in v2:
time: 78.1 us; the launch traced here: 77.9 us
  Pallas kernels  69.9 us (90%)
  local copies, waits for them, and re-layouts  8 us (10%)
    pallas_call x1, Pallas kernels, on_device(): pl.pallas_call(functools.partial(kernel, axes), out_shape=jax.ShapeDtypeS...  69.9 us
    unnamed x3, local copies, waits for them, and re-layouts  8 us

profile of v2, /device:TPU:1, one launch (start us, length us, event | category | flops | bytes accessed | tf_op | source)
XLA Modules:
  0.0 77.9 jit_solution(2905804538508797376)
XLA Ops:
  0.0 1.8 %copy.7.taps_ref = f32[1,7,8192]{2,1,0:T(8,128)} copy(f32[1,7,8192]{2,0,1:T(1,128)} %param.8) | data formatting | bytes 458752 | tf_op args[3]
  1.8 2.3 %copy.6.feat_ref = f32[1,2,3,3,8192]{4,3,2,1,0:T(4,128)} copy(f32[1,2,3,3,8192]{4,1,3,2,0:T(2,128)} %param.7) | data formatting | bytes 1179648 | tf_op args[2]
  4.1 69.9 %pair.1 = bf16[192,8192]{1,0:T(8,128)(2,1)} custom-call(bf16[192,8192]{1,0:T(8,128)(2,1)} %x_ref.1, f32[1,2,8192]{2,1,0:T(2,128)} %gain_ref.1, f32[1,2,3,3,8192]{4,3,2,1,0:T(4,128)} %copy.6.feat_ref, f32[1,7,8192]{2,1,0:T(8,128)} %copy.7.taps_ref, bf16[1,128,512]{2,1,0:T(8,128)(2,1)} %mr_ref.1), custom_call_target="tpu_custom_call" | custom-call | tf_op jit(solution)/shard_map/pair/pallas_call | solution.py:241
  74.0 3.9 %copy.9 = bf16[192,8192]{1,0:T(8,128)(2,1)} copy(bf16[192,8192]{1,0:T(8,128)(2,1)} %pair.1) | data formatting | bytes 6291456

commit v3 on v2

v3 whole, which is shorter than its diff:
```python
import functools

import jax
import jax.numpy as jnp
from jax import lax
from jax.experimental import pallas as pl
from jax.experimental.pallas import tpu as pltpu
from jax.sharding import PartitionSpec as P

F32 = jnp.float32
BF16 = jnp.bfloat16
LANES = 128
CHUNKS = 16
EARLY = 4
STEP = 4
LEAD = 16
MESH = pl.DeviceIdType.MESH


def lanes_of(c, width=LANES):
    return pl.ds(pl.multiple_of(c * width, width), width)


def row_scale(total, channels):
    mean = jnp.sum(total, axis=-1, keepdims=True) * (1.0 / channels)
    return jnp.broadcast_to(lax.rsqrt(mean + 1e-06), total.shape)


def square_sums(read, rows, blocks):
    def add(c, total):
        v = read(c).astype(F32)
        return total + v * v

    return lax.fori_loop(0, blocks, add, jnp.zeros((rows, LANES), F32))


def stream(z_ref, taps, first, rows):
    total = taps[0] * z_ref[8 + first : 8 + first + rows]
    for i in range(1, len(taps)):
        total = total + taps[i] * z_ref[8 + first - i : 8 + first - i + rows]
    return total


def feat_rows(feat_ref, o, gain, cs):
    streams, feat = feat_ref.shape[1:3]
    return [[feat_ref[0, j, i, o : o + 1, cs] * gain for i in range(feat)] for j in range(streams)]


def pieces(rows, most=48):
    return [(first, min(most, rows - first)) for first in range(0, rows, most)]


def short_block(c, read, rows, start, gain_ref, feat_ref, taps_ref, h_ref, z_ref, w_ref, s_ref, sum_ref):
    cs = lanes_of(c)
    gain = gain_ref[0, 0:1, cs]
    taps = feat_rows(feat_ref, 0, gain, cs)
    short = [taps_ref[i, 0:1, cs] for i in range(taps_ref.shape[0])]
    z_ref[8 : 8 + rows] = read(c).astype(F32) * s_ref[:rows]
    for first, count in pieces(rows):
        u1 = stream(z_ref, taps[1], first, count)
        u2 = stream(z_ref, taps[2], first, count)
        w_ref[8 + first : 8 + first + count] = (u1 * u2).astype(BF16).astype(F32)
    for first, count in pieces(rows):
        f = stream(w_ref, short, first, count)
        u0 = stream(z_ref, taps[0], first, count)
        h_ref[start + first : start + first + count, cs] = u0 * f
    h = (h_ref[start : start + rows, cs] + read(c).astype(F32)).astype(BF16).astype(F32)
    h_ref[start : start + rows, cs] = h
    sum_ref[:rows] += h * h


def kernel(axes, x_ref, gain_ref, feat_ref, taps_ref, mr_ref, out_ref,
           lead_ref, win_ref, h_ref, u_ref, table_ref, base_ref, rhs_ref, scale_ref, z_ref, w_ref,
           s_ref, sum_ref, tell_ref, told_ref, give_ref, got_ref, lead_sems, send_sems, recv_sems):
    rows, channels = x_ref.shape
    tap_count, group_count = mr_ref.shape[1:]
    per_group = channels // group_count
    groups = LANES // per_group
    half = rows // 2
    blocks = channels // LANES
    part = channels // CHUNKS
    outer, inner = axes
    inner_size = lax.axis_size(inner)
    count = lax.axis_size(outer) * inner_size
    me = lax.axis_index(outer) * inner_size + lax.axis_index(inner)
    behind, ahead = me - 1, me + 1
    has_behind, has_ahead = me > 0, me < count - 1

    def place(index):
        return (index // inner_size, index % inner_size)

    barrier = pltpu.get_barrier_semaphore()

    @pl.when(has_behind)
    def _():
        pl.semaphore_signal(barrier, inc=1, device_id=place(behind), device_id_type=MESH)

    @pl.when(has_ahead)
    def _():
        pl.semaphore_signal(barrier, inc=1, device_id=place(ahead), device_id_type=MESH)

    peers = has_behind.astype(jnp.int32) + has_ahead.astype(jnp.int32)
    pl.semaphore_wait(barrier, peers)

    def lead_copy():
        return pltpu.make_async_remote_copy(
            src_ref=x_ref.at[pl.ds(rows - LEAD, LEAD)], dst_ref=lead_ref,
            send_sem=lead_sems.at[0], recv_sem=lead_sems.at[1],
            device_id=place(ahead), device_id_type=MESH)

    def part_copy(k):
        cs = lanes_of(k, part)
        return pltpu.make_async_remote_copy(
            src_ref=win_ref.at[pl.ds(rows, tap_count), cs],
            dst_ref=win_ref.at[pl.ds(0, tap_count), cs],
            send_sem=send_sems.at[k], recv_sem=recv_sems.at[k],
            device_id=place(ahead), device_id_type=MESH)

    tail = tap_count + LEAD

    def tell_copy():
        return pltpu.make_async_remote_copy(
            src_ref=tell_ref, dst_ref=told_ref,
            send_sem=lead_sems.at[2], recv_sem=lead_sems.at[3],
            device_id=place(ahead), device_id_type=MESH)

    def early_copy(k):
        cs = lanes_of(k, part)
        return pltpu.make_async_remote_copy(
            src_ref=give_ref.at[:, cs], dst_ref=got_ref.at[:, cs],
            send_sem=send_sems.at[k], recv_sem=recv_sems.at[k],
            device_id=place(ahead), device_id_type=MESH)

    @pl.when(has_ahead)
    def _():
        lead_copy().start()

    z_ref[...] = jnp.zeros_like(z_ref)
    w_ref[...] = jnp.zeros_like(w_ref)
    share = (gain_ref, feat_ref, taps_ref, h_ref, z_ref, w_ref, s_ref, sum_ref)
    here = blocks // CHUNKS
    early_blocks = EARLY * here

    def mr_product(taps, first, size):
        return (stream(z_ref, taps[1], first, size) * stream(z_ref, taps[2], first, size)).astype(BF16)

    def mr_taps_of(cs):
        return feat_rows(feat_ref, 1, gain_ref[0, 1:2, cs], cs)

    first_tail = rows - tail
    read_tail = lambda c: x_ref[first_tail:, lanes_of(c)]
    s_ref[:tail] = row_scale(square_sums(read_tail, tail, blocks), channels)
    sum_ref[:tail] = jnp.zeros((tail, LANES), F32)
    start_tail = LEAD + first_tail

    @pl.loop(0, CHUNKS)
    def _(k):
        @pl.loop(0, here)
        def _(b):
            c = k * here + b
            short_block(c, read_tail, tail, start_tail, *share)

            @pl.when(k < EARLY)
            def _():
                give_ref[:, lanes_of(c)] = h_ref[start_tail : start_tail + tail, lanes_of(c)].astype(BF16)

        @pl.when(has_ahead & (k > 0) & (k <= EARLY))
        def _():
            early_copy(k - 1).start()

    scale_ref[start_tail : start_tail + tail] = row_scale(sum_ref[:tail], channels)
    tell_ref[...] = scale_ref[start_tail : start_tail + tail]
    first_sent = rows - tap_count

    @pl.loop(EARLY, CHUNKS)
    def _(k):
        @pl.loop(0, here)
        def _(b):
            cs = lanes_of(k * here + b)
            taps = mr_taps_of(cs)
            n = tap_count + 8
            top = LEAD + first_sent - 8
            z_ref[0:n] = h_ref[top : top + n, cs] * scale_ref[top : top + n]
            for first, size in pieces(tap_count):
                win_ref[rows + first : rows + first + size, cs] = mr_product(taps, first, size)

        @pl.when(has_ahead & (k == EARLY))
        def _():
            tell_copy().start()

        @pl.when(has_ahead & (k > EARLY))
        def _():
            part_copy(k - 1).start()

    at_tap = lax.broadcasted_iota(jnp.int32, (tap_count, tap_count), 0)
    at_lag = lax.broadcasted_iota(jnp.int32, (tap_count, tap_count), 1)
    flip = jnp.where((at_tap + at_lag == tap_count) | (at_tap + at_lag == 0), 1.0, 0.0).astype(BF16)
    past = (lax.broadcasted_iota(jnp.int32, (half, tap_count), 1)
            > lax.broadcasted_iota(jnp.int32, (half, tap_count), 0))
    base_ref[...] = lax.dot_general(mr_ref[0], flip, (((0,), (0,)), ((), ())),
                                    preferred_element_type=F32)
    rhs_ref[...] = jnp.zeros_like(rhs_ref)

    @pl.when(has_ahead)
    def _():
        part_copy(CHUNKS - 1).start()

    @pl.when(has_behind)
    def _():
        lead_copy().wait_recv()

    @pl.when(jnp.logical_not(has_behind))
    def _():
        lead_ref[...] = jnp.zeros_like(lead_ref)
        win_ref[:tap_count] = jnp.zeros((tap_count, channels), BF16)

    head = LEAD + first_sent
    z_ref[0:8] = jnp.zeros((8, LANES), F32)
    read_head = lambda c: jnp.concatenate(
        [lead_ref[:, lanes_of(c)], x_ref[:first_sent, lanes_of(c)]], axis=0)
    s_ref[:head] = row_scale(square_sums(read_head, head, blocks), channels)
    sum_ref[:head] = jnp.zeros((head, LANES), F32)

    @pl.loop(0, blocks)
    def _(c):
        short_block(c, read_head, head, 0, *share)

    scale_ref[:head] = row_scale(sum_ref[:head], channels)

    @pl.loop(0, blocks)
    def _(c):
        cs = lanes_of(c)
        taps = mr_taps_of(cs)
        z_ref[0 : rows + 8] = h_ref[LEAD - 8 :, cs] * scale_ref[LEAD - 8 :]

        def put(low, high):
            for first, size in pieces(high - low):
                first += low
                win_ref[tap_count + first : tap_count + first + size, cs] = mr_product(taps, first, size)

        put(0, first_sent)

        @pl.when(c < early_blocks)
        def _():
            put(first_sent, rows)

        for first, size in pieces(rows):
            u_ref[first : first + size, cs] = stream(z_ref, taps[0], first, size)

    @pl.loop(0, blocks)
    def _(c):
        lags = base_ref[pl.ds(pl.multiple_of(c * groups, groups), groups), :]
        for g in range(groups):
            row = jnp.broadcast_to(lags[g : g + 1], (half, tap_count))
            turned = pltpu.roll(row, 0, 1, stride=1, stride_axis=0)
            gs = slice(g * half, (g + 1) * half)
            table_ref[c, gs, :tap_count] = jnp.where(past, turned, 0.0).astype(BF16)
            table_ref[c, gs, tap_count:] = jnp.where(past, 0.0, turned).astype(BF16)

    lane_group = lax.broadcasted_iota(jnp.int32, (half, LANES), 1) // per_group
    reach = half + tap_count

    @pl.loop(0, CHUNKS)
    def _(k):
        @pl.when(has_behind & (k == 0))
        def _():
            tell_copy().wait_recv()

        @pl.when(has_behind & (k < EARLY))
        def _():
            early_copy(k).wait_recv()

            @pl.loop(0, here)
            def _(b):
                cs = lanes_of(k * here + b)
                taps = mr_taps_of(cs)
                z_ref[0:tail] = got_ref[:, cs].astype(F32) * told_ref[...]
                for first, size in pieces(tap_count):
                    win_ref[first : first + size, cs] = mr_product(taps, tail - tap_count - 8 + first, size)

        @pl.when(has_behind & (k >= EARLY))
        def _():
            part_copy(k).wait_recv()

        @pl.loop(0, blocks // CHUNKS, step=STEP)
        def _(b):
          for slot in range(STEP):
            c = k * (blocks // CHUNKS) + b + slot
            cs = lanes_of(c)
            rhs_ref[slot, :reach, :LANES] = win_ref[:reach, cs]
            rhs_ref[slot, :reach, LANES:] = win_ref[half : half + reach, cs]
            product = jnp.dot(table_ref[c], rhs_ref[slot], preferred_element_type=F32)
            for side in range(2):
                ls = slice(side * LANES, (side + 1) * LANES)
                f = product[0:half, ls]
                for g in range(1, groups):
                    f = jnp.where(lane_group == g, product[g * half : (g + 1) * half, ls], f)
                rs = slice(side * half, (side + 1) * half)
                hs = slice(LEAD + side * half, LEAD + (side + 1) * half)
                out_ref[rs, cs] = (h_ref[hs, cs] + u_ref[rs, cs] * f).astype(BF16)

    @pl.when(has_ahead)
    def _():
        lead_copy().wait_send()

        tell_copy().wait_send()

        @pl.loop(0, EARLY)
        def _(k):
            early_copy(k).wait_send()

        @pl.loop(EARLY, CHUNKS)
        def _(k):
            part_copy(k).wait_send()


def on_device(axes, tokens, norm_gain, feat_taps, se_taps, mr_taps):
    rows, channels = tokens.shape
    tap_count, group_count = mr_taps.shape[1:]
    groups = LANES * group_count // channels
    blocks = channels // LANES
    spread = 2 * tap_count
    return pl.pallas_call(
        functools.partial(kernel, axes),
        out_shape=jax.ShapeDtypeStruct((rows, channels), BF16),
        in_specs=[pl.BlockSpec(memory_space=pltpu.VMEM)] * 5,
        out_specs=pl.BlockSpec(memory_space=pltpu.VMEM),
        scratch_shapes=[
            pltpu.VMEM((LEAD, channels), BF16),
            pltpu.VMEM((tap_count + rows, channels), BF16),
            pltpu.VMEM((LEAD + rows, channels), F32),
            pltpu.VMEM((rows, channels), F32),
            pltpu.VMEM((blocks, groups * rows // 2, spread), BF16),
            pltpu.VMEM((group_count, tap_count), F32),
            pltpu.VMEM((STEP, spread, 2 * LANES), BF16),
            pltpu.VMEM((LEAD + rows, LANES), F32),
            pltpu.VMEM((LEAD + rows, LANES), F32),
            pltpu.VMEM((LEAD + rows, LANES), F32),
            pltpu.VMEM((LEAD + rows, LANES), F32),
            pltpu.VMEM((LEAD + rows, LANES), F32),
            pltpu.VMEM((tap_count + LEAD, LANES), F32),
            pltpu.VMEM((tap_count + LEAD, LANES), F32),
            pltpu.VMEM((tap_count + LEAD, EARLY * channels // CHUNKS), BF16),
            pltpu.VMEM((tap_count + LEAD, EARLY * channels // CHUNKS), BF16),
            pltpu.SemaphoreType.DMA((4,)),
            pltpu.SemaphoreType.DMA((CHUNKS,)),
            pltpu.SemaphoreType.DMA((CHUNKS,)),
        ],
        compiler_params=pltpu.CompilerParams(
            collective_id=0, has_side_effects=True, vmem_limit_bytes=67043328),
        name="pair",
    )(tokens, norm_gain, feat_taps.transpose(0, 2, 3, 1, 4), se_taps.transpose(1, 0, 2), mr_taps)


def solution(mesh):
    axes = tuple(mesh.axis_names)
    placed = (P(axes, None), P(), P(), P(), P())
    return jax.shard_map(
        functools.partial(on_device, axes),
        mesh=mesh,
        in_specs=placed,
        out_specs=P(axes, None),
        check_vma=False,
    )
```

time: 78.1 us -> 72.2 us (0.924)
  local copies, waits for them, and re-layouts: 8 us -> 3.86 us
  Pallas kernels: 69.9 us -> 68.2 us
    unnamed x3 -> x1, local copies, waits for them, and re-layouts: 8 us -> 3.86 us
    pallas_call x1, Pallas kernels: 69.9 us -> 68.2 us  [on_device(): pl.pallas_call(functools.partial(kernel, axes), out_shape=jax.ShapeDtypeS...]
where the time goes in v3:
time: 72.2 us; the launch traced here: 72.1 us
  Pallas kernels  68.2 us (94%)
  local copies, waits for them, and re-layouts  3.86 us (5%)
    pallas_call x1, Pallas kernels, on_device(): pl.pallas_call(functools.partial(kernel, axes), out_shape=jax.ShapeDtypeS...  68.2 us
    unnamed x1, local copies, waits for them, and re-layouts  3.86 us

profile of v3, /device:TPU:1, one launch (start us, length us, event | category | flops | bytes accessed | tf_op | source)
XLA Modules:
  0.0 72.1 jit_solution(8537745686319987501)
XLA Ops:
  0.0 68.2 %pair.1 = bf16[192,8192]{1,0:T(8,128)(2,1)} custom-call(bf16[192,8192]{1,0:T(8,128)(2,1)} %x_ref.1, f32[1,2,8192]{2,1,0:T(2,128)} %gain_ref.1, f32[1,3,3,2,8192]{4,3,2,1,0:T(2,128)} %bitcast.2, f32[7,1,8192]{2,1,0:T(1,128)} %bitcast.3, bf16[1,128,512]{2,1,0:T(8,128)(2,1)} %mr_ref.1), custom_call_target="tpu_custom_call" | custom-call | tf_op jit(solution)/shard_map/pair/pallas_call | solution.py:323
  68.2 3.9 %copy.7 = bf16[192,8192]{1,0:T(8,128)(2,1)} copy(bf16[192,8192]{1,0:T(8,128)(2,1)} %pair.1) | data formatting | bytes 6291456
